TPU v7x, 128 devices: a whole 4x4x4 slice. The times are simulated.
128 devices in a mesh: seq: 32 (over z, x, core), dp: 4 (over y).
Axes of the slice: x: 4, y: 4, z: 4, core: 2. Of those that a mesh axis runs over, the one named last changes fastest.
Arguments:
- queries: bfloat16 [4, 8192, 1024], P('dp', 'seq'), may hold values from -8 to 8
- key_rows: bfloat16 [4, 8192, 1024], P('dp', 'seq'), may hold values from -8 to 8
- value_rows: bfloat16 [4, 8192, 1024], P('dp', 'seq'), may hold values from -16 to 16
- conv_key: float32 [5, 4, 1024], replicated, may hold values from -2.5 to 2.5
- conv_value: float32 [5, 4, 1024], replicated, may hold values from -2.5 to 2.5
- grad_out: bfloat16 [4, 8192, 1024], P('dp', 'seq'), may hold values from -12 to 12
Outputs:
- attended: bfloat16 [4, 8192, 1024], P('dp', 'seq')
- grad_query: bfloat16 [4, 8192, 1024], P('dp', 'seq')
- grad_key: bfloat16 [4, 8192, 1024], P('dp', 'seq')
- grad_value: bfloat16 [4, 8192, 1024], P('dp', 'seq')
- grad_conv_key: float32 [5, 4, 1024], replicated
- grad_conv_value: float32 [5, 4, 1024], replicated
All inputs are finite; a program needn't handle non-finite values.
Results may differ from a plain program's by a relative error of at most 0.019.
Values may be sent and summed in bfloat16 or wider, within the bound.
No kernel may reach another device: no remote copies, remote signals or barrier semaphores. Data moves between devices by JAX's collectives and lax.ppermute only.
A program may use at most 128 MiB of HBM per device.

v0:
```python
import jax
import jax.numpy as jnp
from jax import lax
from jax.sharding import PartitionSpec as P

HEADS = 8
HEAD_DIM = 128
BLOCK = 128


def passed_along(value, axis, steps):
    count = lax.axis_size(axis)
    initial, last = (max(0, -steps), min(count, count - steps))
    return lax.ppermute(value, axis, [(source, source + steps) for source in range(initial, last)])


def partner_2(array, axis, distance):
    return lax.ppermute(array, axis, [(i, i ^ 1 << distance) for i in range(lax.axis_size(axis))])


def coarsen(extended, weight):
    out_rows = (extended.shape[1] - 2) // 2
    summed = weight[0] * extended[:, 0 : 2 * out_rows : 2].astype(jnp.float32)
    for offset in range(1, 4):
        summed = summed + weight[offset] * extended[:, offset : offset + 2 * out_rows : 2].astype(
            jnp.float32
        )
    return summed.astype(jnp.bfloat16)


def coarsen_back(upstream, extended, weight):
    seqs_dev, out_rows, feat_width = upstream.shape
    zero_row = jnp.zeros((seqs_dev, 1, feat_width), jnp.float32)
    even_rows = jnp.concatenate([weight[0] * upstream, zero_row], 1) + jnp.concatenate(
        [zero_row, weight[2] * upstream], 1
    )
    odd_rows = jnp.concatenate([weight[1] * upstream, zero_row], 1) + jnp.concatenate(
        [zero_row, weight[3] * upstream], 1
    )
    spread = jnp.stack([even_rows, odd_rows], 2).reshape(seqs_dev, 2 * out_rows + 2, feat_width)
    weight_grad = jnp.stack(
        [
            jnp.sum(
                upstream * extended[:, offset : offset + 2 * out_rows : 2].astype(jnp.float32),
                (0, 1),
            )
            for offset in range(4)
        ]
    )
    return (spread, weight_grad)


def move_near(moved_rows, shift_by):
    return passed_along(moved_rows, "seq", shift_by)


def move_grads(moved_rows, shift_by):
    return passed_along(moved_rows.astype(jnp.bfloat16), "seq", shift_by).astype(moved_rows.dtype)


def per_device(queries, key_rows, value_rows, conv_key, conv_value, grad_out):
    seqs_dev, tok_rows, feat_width = queries.shape
    levels = conv_key.shape[0]
    head_count = HEADS
    head_size = HEAD_DIM
    blk_rows = BLOCK
    blocks_here = tok_rows // blk_rows
    local_top = blocks_here.bit_length() - 1
    seq_devices = lax.axis_size("seq")
    dev_index = lax.axis_index("seq")
    total_blocks = blocks_here * seq_devices
    score_scale = head_size ** (-0.5)
    pair_width = 2 * feat_width
    group_heads = 2
    kv_weight = jnp.stack(
        [
            conv_key.reshape(levels, 4, head_count, head_size),
            conv_value.reshape(levels, 4, head_count, head_size),
        ],
        3,
    ).reshape(levels, 4, pair_width)
    fine_pairs = jnp.stack(
        [
            key_rows.reshape(seqs_dev, tok_rows, head_count, head_size),
            value_rows.reshape(seqs_dev, tok_rows, head_count, head_size),
        ],
        3,
    ).reshape(seqs_dev, tok_rows, pair_width)
    own_rows = [fine_pairs]
    left_rims = [move_near(fine_pairs[:, -blk_rows:], 1)]
    right_rims = [move_near(fine_pairs[:, :blk_rows], -1)]
    extended_local = [None]
    level_id = 1
    extended = jnp.concatenate([left_rims[level_id - 1][:, -2:], own_rows[level_id - 1]], 1)
    extended_local.append(extended)
    coarse = coarsen(extended, kv_weight[level_id - 1])
    own_rows.append(coarse)
    left_rims.append(move_near(coarse, 1))
    right_rims.append(move_near(coarse, -1))
    block_now = own_rows[local_top]
    left_now = left_rims[local_top]
    group_lefts, group_rights, group_extended, group_first = ([], [], [], [])
    for level_id in range(local_top + 1, levels + 1):
        swap_bit = level_id - local_top - 1
        extended = jnp.concatenate([left_now[:, -2:], block_now], 1)
        group_extended.append(extended)
        own_half = coarsen(extended, kv_weight[level_id - 1])
        partner = partner_2(own_half, "seq", swap_bit)
        is_first = dev_index // 2**swap_bit % 2 == 0
        group_first.append(is_first)
        block_now = jnp.where(
            is_first,
            jnp.concatenate([own_half, partner], 1),
            jnp.concatenate([partner, own_half], 1),
        )
        stride_dev = 2 ** (level_id - local_top)
        left_now = move_near(block_now, stride_dev)
        right_now = move_near(block_now, -stride_dev)
        group_lefts.append(left_now)
        group_rights.append(right_now)
    glob_blocks = dev_index * blocks_here + jnp.arange(blocks_here, dtype=jnp.int32)
    always = jnp.ones((blocks_here,), jnp.bool_)
    sources = []
    pieces = []
    for level_id in range(local_top + 1):
        block_count = blocks_here >> level_id
        padded = jnp.concatenate([left_rims[level_id], own_rows[level_id], right_rims[level_id]], 1)
        sources.append(
            padded.reshape(seqs_dev, block_count + 2, blk_rows, head_count, 2, head_size)
        )
        coarse_id = glob_blocks // 2**level_id
        spread = 2**level_id
        pieces.append((level_id, 0, spread, coarse_id >= 1))
        if level_id == 0:
            pieces.append((0, 1, 1, always))
        pieces.append((level_id, 2, spread, coarse_id + 1 < total_blocks // 2**level_id))
    for slot_id in range(levels - local_top):
        level_id = local_top + 1 + slot_id
        coarse_id = glob_blocks // 2**level_id
        sources.append(
            group_lefts[slot_id].reshape(seqs_dev, 1, blk_rows, head_count, 2, head_size)
        )
        pieces.append((len(sources) - 1, 0, blocks_here, coarse_id >= 1))
        sources.append(
            group_rights[slot_id].reshape(seqs_dev, 1, blk_rows, head_count, 2, head_size)
        )
        pieces.append(
            (len(sources) - 1, 0, blocks_here, coarse_id + 1 < total_blocks // 2**level_id)
        )
    query_blocks = queries.reshape(seqs_dev, blocks_here, blk_rows, head_count, head_size)
    out_blocks = grad_out.reshape(seqs_dev, blocks_here, blk_rows, head_count, head_size)

    def head_group(group_id, loop_state):
        attended_acc, grad_q_acc, source_grads, log_totals, row_deltas = loop_state
        head_start = group_id * group_heads
        q_part = lax.dynamic_slice_in_dim(query_blocks, head_start, group_heads, 3)
        do_part = lax.dynamic_slice_in_dim(out_blocks, head_start, group_heads, 3)
        source_parts = [
            lax.dynamic_slice_in_dim(source, head_start, group_heads, 3) for source in sources
        ]
        score_list = []
        views = []
        for source_id, offset, spread, valid_mask in pieces:
            block_count = blocks_here // spread
            key_blocks = source_parts[source_id][:, offset : offset + block_count]
            q_view = q_part.reshape(seqs_dev, block_count, spread, blk_rows, group_heads, head_size)
            do_view = do_part.reshape(
                seqs_dev, block_count, spread, blk_rows, group_heads, head_size
            )
            raw_scores = jnp.einsum(
                "bnrqhe,bnkhe->bnrhqk",
                q_view,
                key_blocks[..., 0, :],
                preferred_element_type=jnp.float32,
            )
            raw_scores = (
                raw_scores.reshape(seqs_dev, blocks_here, group_heads, blk_rows, blk_rows)
                * score_scale
            )
            score_list.append(
                jnp.where(valid_mask[None, :, None, None, None], raw_scores, -jnp.inf)
            )
            views.append((key_blocks, q_view, do_view, block_count, spread))
        all_scores = jnp.concatenate(score_list, 4)
        row_max = jnp.max(all_scores, 4, keepdims=True)
        exp_scores = jnp.exp(all_scores - row_max)
        summed = jnp.sum(exp_scores, 4, keepdims=True)
        prob_full = exp_scores / summed
        probs_low = prob_full.astype(jnp.bfloat16)
        attended_part = jnp.zeros(
            (seqs_dev, blocks_here, blk_rows, group_heads, head_size), jnp.float32
        )
        grad_prob_list = []
        for piece_id, (key_blocks, q_view, do_view, block_count, spread) in enumerate(views):
            p_slice = probs_low[..., piece_id * blk_rows : (piece_id + 1) * blk_rows].reshape(
                seqs_dev, block_count, spread, group_heads, blk_rows, blk_rows
            )
            attended_part = attended_part + jnp.einsum(
                "bnrhqk,bnkhe->bnrqhe",
                p_slice,
                key_blocks[..., 1, :],
                preferred_element_type=jnp.float32,
            ).reshape(attended_part.shape)
            grad_prob = jnp.einsum(
                "bnrqhe,bnkhe->bnrhqk",
                do_view,
                key_blocks[..., 1, :],
                preferred_element_type=jnp.float32,
            )
            grad_prob_list.append(
                grad_prob.reshape(seqs_dev, blocks_here, group_heads, blk_rows, blk_rows)
            )
        grad_prob_all = jnp.concatenate(grad_prob_list, 4)
        row_delta = jnp.sum(prob_full * grad_prob_all, 4, keepdims=True)
        dscore = (prob_full * (grad_prob_all - row_delta) * score_scale).astype(jnp.bfloat16)
        grad_q_part = jnp.zeros(
            (seqs_dev, blocks_here, blk_rows, group_heads, head_size), jnp.float32
        )
        group_grads = [jnp.zeros(part_arr.shape, jnp.float32) for part_arr in source_parts]
        for piece_id, (key_blocks, q_view, do_view, block_count, spread) in enumerate(views):
            source_id, offset = (pieces[piece_id][0], pieces[piece_id][1])
            p_slice = probs_low[..., piece_id * blk_rows : (piece_id + 1) * blk_rows].reshape(
                seqs_dev, block_count, spread, group_heads, blk_rows, blk_rows
            )
            ds_slice = dscore[..., piece_id * blk_rows : (piece_id + 1) * blk_rows].reshape(
                seqs_dev, block_count, spread, group_heads, blk_rows, blk_rows
            )
            grad_q_part = grad_q_part + jnp.einsum(
                "bnrhqk,bnkhe->bnrqhe",
                ds_slice,
                key_blocks[..., 0, :],
                preferred_element_type=jnp.float32,
            ).reshape(grad_q_part.shape)
            key_grad = jnp.einsum(
                "bnrhqk,bnrqhe->bnkhe", ds_slice, q_view, preferred_element_type=jnp.float32
            )
            value_grad = jnp.einsum(
                "bnrhqk,bnrqhe->bnkhe", p_slice, do_view, preferred_element_type=jnp.float32
            )
            pair_grad = jnp.stack([key_grad, value_grad], 4)
            group_grads[source_id] = (
                group_grads[source_id].at[:, offset : offset + block_count].add(pair_grad)
            )
        attended_acc = lax.dynamic_update_slice_in_dim(
            attended_acc, attended_part.astype(jnp.bfloat16), head_start, 3
        )
        grad_q_acc = lax.dynamic_update_slice_in_dim(
            grad_q_acc, grad_q_part.astype(jnp.bfloat16), head_start, 3
        )
        source_grads = tuple(
            (
                lax.dynamic_update_slice_in_dim(whole, group_part, head_start, 3)
                for whole, group_part in zip(source_grads, group_grads)
            )
        )
        log_totals = lax.dynamic_update_slice_in_dim(
            log_totals, (row_max + jnp.log(summed))[..., 0], head_start, 2
        )
        row_deltas = lax.dynamic_update_slice_in_dim(row_deltas, row_delta[..., 0], head_start, 2)
        return (attended_acc, grad_q_acc, source_grads, log_totals, row_deltas)

    start_state = (
        jnp.zeros((seqs_dev, blocks_here, blk_rows, head_count, head_size), jnp.bfloat16),
        jnp.zeros((seqs_dev, blocks_here, blk_rows, head_count, head_size), jnp.bfloat16),
        tuple((jnp.zeros(source.shape, jnp.float32) for source in sources)),
        jnp.zeros((seqs_dev, blocks_here, head_count, blk_rows), jnp.float32),
        jnp.zeros((seqs_dev, blocks_here, head_count, blk_rows), jnp.float32),
    )
    attended_acc, grad_q_acc, source_grads, log_totals, row_deltas = lax.fori_loop(
        0, head_count // group_heads, head_group, start_state
    )
    attended = attended_acc.reshape(seqs_dev, tok_rows, feat_width)
    grad_query = grad_q_acc.reshape(seqs_dev, tok_rows, feat_width)
    grad_left, grad_own, grad_right = ([], [], [])
    for level_id in range(local_top + 1):
        flat_grad = source_grads[level_id].reshape(seqs_dev, -1, pair_width)
        grad_left.append(flat_grad[:, :blk_rows])
        grad_own.append(flat_grad[:, blk_rows:-blk_rows])
        grad_right.append(flat_grad[:, -blk_rows:])
    group_left_grads = [
        source_grads[local_top + 1 + 2 * slot_id].reshape(seqs_dev, blk_rows, pair_width)
        for slot_id in range(levels - local_top)
    ]
    group_right_grads = [
        source_grads[local_top + 2 + 2 * slot_id].reshape(seqs_dev, blk_rows, pair_width)
        for slot_id in range(levels - local_top)
    ]
    weight_grads = [None] * levels
    carry_block = jnp.zeros((seqs_dev, blk_rows, pair_width), jnp.float32)
    carry_left = jnp.zeros((seqs_dev, 2, pair_width), jnp.float32)
    for level_id in range(levels, local_top, -1):
        slot_id = level_id - local_top - 1
        stride_dev = 2 ** (level_id - local_top)
        left_total = group_left_grads[slot_id].at[:, -2:].add(carry_left)
        block_total = (
            carry_block
            + move_grads(left_total, -stride_dev)
            + move_grads(group_right_grads[slot_id], stride_dev)
        )
        first_part = block_total[:, : blk_rows // 2]
        second_part = block_total[:, blk_rows // 2 :]
        keep_part = jnp.where(group_first[slot_id], first_part, second_part)
        give_part = jnp.where(group_first[slot_id], second_part, first_part)
        half_grad = keep_part + partner_2(give_part.astype(jnp.bfloat16), "seq", slot_id).astype(
            give_part.dtype
        )
        spread, weight_grads[level_id - 1] = coarsen_back(
            half_grad, group_extended[slot_id], kv_weight[level_id - 1]
        )
        carry_left = spread[:, :2]
        carry_block = spread[:, 2:]
    grad_left[local_top] = grad_left[local_top].at[:, -2:].add(carry_left)
    grad_own[local_top] = grad_own[local_top] + carry_block
    fine_left_conv = jnp.zeros((seqs_dev, blk_rows, pair_width), jnp.float32)
    level_id = 1
    from_right = move_grads(grad_left[level_id], -1)
    from_left = move_grads(grad_right[level_id], 1)
    level_grad = (
        grad_own[level_id].at[:, :blk_rows].add(from_left).at[:, -blk_rows:].add(from_right)
    )
    spread, weight_grads[level_id - 1] = coarsen_back(
        level_grad, extended_local[level_id], kv_weight[level_id - 1]
    )
    fine_left_conv = fine_left_conv.at[:, -2:].add(spread[:, :2])
    grad_own[level_id - 1] = grad_own[level_id - 1] + spread[:, 2:]
    from_right = move_grads(grad_left[0] + fine_left_conv, -1)
    from_left = move_grads(grad_right[0], 1)
    fine_grad = grad_own[0].at[:, :blk_rows].add(from_left).at[:, -blk_rows:].add(from_right)
    grad_pairs = fine_grad.reshape(seqs_dev, tok_rows, head_count, 2, head_size)
    grad_key = (
        grad_pairs[:, :, :, 0, :].reshape(seqs_dev, tok_rows, feat_width).astype(jnp.bfloat16)
    )
    grad_value = (
        grad_pairs[:, :, :, 1, :].reshape(seqs_dev, tok_rows, feat_width).astype(jnp.bfloat16)
    )
    weight_sum = lax.psum(jnp.stack(weight_grads), ("seq", "dp")).reshape(
        levels, 4, head_count, 2, head_size
    )
    grad_conv_key = weight_sum[:, :, :, 0, :].reshape(levels, 4, feat_width)
    grad_conv_value = weight_sum[:, :, :, 1, :].reshape(levels, 4, feat_width)
    return (attended, grad_query, grad_key, grad_value, grad_conv_key, grad_conv_value)


def solution(mesh):
    in_specs = (
        P("dp", "seq", None),
        P("dp", "seq", None),
        P("dp", "seq", None),
        P(),
        P(),
        P("dp", "seq", None),
    )
    out_specs = (
        P("dp", "seq", None),
        P("dp", "seq", None),
        P("dp", "seq", None),
        P("dp", "seq", None),
        P(),
        P(),
    )
    return jax.shard_map(
        per_device, mesh=mesh, in_specs=in_specs, out_specs=out_specs, check_vma=False
    )
```

profile of v0, /device:TPU:1, one launch (start us, length us, event | category | flops | bytes accessed | tf_op | source)
XLA Modules:
  0.0 1245.0 jit_solution(9767372504227561443)
XLA Ops:
  15.2 20.2 %slice.1813 = bf16[1,128,2048]{1,2,0:T(8,128)(2,1)S(1)} slice(bf16[1,256,2048]{1,2,0:T(8,128)(2,1)S(1)} %bitcast.1716), slice={[0:1:1], [0:256:2], [0:2048:1]} | slice | bytes 1048576 | tf_op jit(solution)/shard_map/slice | solution.py:25
  35.5 20.2 %slice.1815 = bf16[1,128,2048]{1,2,0:T(8,128)(2,1)S(1)} slice(bf16[1,256,2048]{1,2,0:T(8,128)(2,1)S(1)} %bitcast.1717), slice={[0:1:1], [1:256:2], [0:2048:1]} | slice | bytes 1048576 | tf_op jit(solution)/shard_map/slice | solution.py:25
  58.7 20.9 %slice.1811 = bf16[1,128,2048]{1,2,0:T(8,128)(2,1)S(1)} slice(bf16[1,258,2048]{1,2,0:T(8,128)(2,1)} %pad_maximum_fusion.14), slice={[0:1:1], [1:257:2], [0:2048:1]} | slice | bytes 1048576 | tf_op jit(solution)/shard_map/slice | solution.py:25
  79.6 21.3 %slice.1809 = bf16[1,128,2048]{1,2,0:T(8,128)(2,1)} slice(bf16[1,258,2048]{1,2,0:T(8,128)(2,1)} %pad_maximum_fusion.14), slice={[0:1:1], [0:256:2], [0:2048:1]} | slice | bytes 1048576 | tf_op jit(solution)/shard_map/slice | solution.py:23
  106.1 11.0 slice.1824
  130.9 11.6 slice.1820
  142.4 11.9 slice.1818
  166.5 11.0 slice.1833
  191.2 11.9 slice.1829
  203.2 11.8 slice.1827
  218.9 12.9 %collective-permute-done.7 = bf16[1,64,2048]{1,2,0:T(8,128)(2,1)S(1)} collective-permute-done((bf16[1,64,2048]{1,2,0:T(8,128)(2,1)}, bf16[1,64,2048]{1,2,0:T(8,128)(2,1)S(1)}, u32[]{:S(2)}, u32[]{:S(2)}) %collective-permute-start.7) | collective-permute-done | bytes 262176 | tf_op jit(solution)/shard_map/ppermute | solution.py:18
  238.8 11.0 slice.1842
  249.8 11.2 slice.1840
  263.7 11.9 slice.1838
  275.6 11.8 slice.1836
  292.2 12.7 %collective-permute-done.10 = bf16[1,64,2048]{1,2,0:T(8,128)(2,1)S(1)} collective-permute-done((bf16[1,64,2048]{1,2,0:T(8,128)(2,1)}, bf16[1,64,2048]{1,2,0:T(8,128)(2,1)S(1)}, u32[]{:S(2)}, u32[]{:S(2)}) %collective-permute-start.10) | collective-permute-done | bytes 262176 | tf_op jit(solution)/shard_map/ppermute | solution.py:18
  317.9 11.5 slice.1851
  329.4 11.8 slice.1849
  344.9 11.9 slice.1847
  356.9 11.8 slice.1845
  426.1 424.3 %while.137 = (s32[]{:T(128)}, bf16[1,2,128,8,128]{4,3,2,1,0:T(8,128)(2,1)}, bf16[1,2,128,8,128]{4,3,2,1,0:T(8,128)(2,1)}, f32[1,4,128,8,2,128]{5,4,3,0,2,1:T(2,1...) while((s32[]{:T(128)}, ...), condition=%wide.region_16.17_spmd.clone.clone, body=%wide.region_0.16_spmd.clone.clone.sunk | while | flops 1327627008 | bytes 139415504 | solution.py:269
  912.0 13.4 %collective-permute-start.21 = (bf16[1,64,2048]{1,2,0:T(8,128)(2,1)S(1)}, bf16[1,64,2048]{1,2,0:T(8,128)(2,1)S(1)}, u32[]{:S(2)}, u32[]{:S(2)}) collective-permute-start(bf16[1,64,2048]{1,2,0:T(8,128)(2,1)S(1)} %select_convert_fusion.2), channel_id=1, source_target_pairs={{0,16},{4,20},{8,24},{12,28},{16,0},{20,4},{24,8},{28,12},{32,48},... | collective-permute-start | bytes 786440 | tf_op jit(solution)/shard_map/ppermute | solution.py:18
  1009.6 17.7 %collective-permute-start.27 = (bf16[1,64,2048]{1,2,0:T(8,128)(2,1)}, bf16[1,64,2048]{1,2,0:T(8,128)(2,1)}, u32[]{:S(2)}, u32[]{:S(2)}) collective-permute-start(bf16[1,64,2048]{1,2,0:T(8,128)(2,1)} %select_convert_fusion), channel_id=1, source_target_pairs={{0,4},{4,0},{8,12},{12,8},{16,20},{20,16},{24,28},{28,24},{32,36},... | collective-permute-start | bytes 786440 | tf_op jit(solution)/shard_map/ppermute | solution.py:18
  1102.5 129.7 %all-reduce.24.cloned.1.call-done = f32[5,4,8,2,128]{4,3,2,1,0:T(2,128)} async-done(((f32[5,4,8,2,128]{4,3,2,1,0:T(2,128)}), f32[5,4,8,2,128]{4,3,2,1,0:T(2,128)}) %all-reduce.24.cloned.1.call-update) | async-done | bytes 163856 | tf_op jit(solution)/shard_map/psum | solution.py:336
  (1195 shorter events, 793.9 us)
Async XLA Ops:
  7.2 1225.0 %all-reduce.24.cloned.1.call-start = ((), (), s32[]{:S(2)}) async-start(), calls=%async_computation | async-start | bytes 327680 | tf_op jit(solution)/shard_map/psum | solution.py:336
  10.7 45.3 %collective-permute-start = (bf16[1,128,2048]{1,2,0:T(8,128)(2,1)S(1)}, bf16[1,128,2048]{1,2,0:T(8,128)(2,1)S(1)}, u32[]{:S(2)}, u32[]{:S(2)}) collective-permute-start(bf16[1,128,2048]{1,2,0:T(8,128)(2,1)S(1)} %get-tuple-element.1887), channel_id=1, source_target_pairs={{0,4},{4,8},{8,12},{12,16},{16,20},{20,24},{24,28},{28,32},{32,36}... | collective-permute-start | bytes 1572872 | tf_op jit(solution)/shard_map/ppermute | solution.py:14
  103.9 24.1 %collective-permute-start.2 = (bf16[1,128,2048]{1,2,0:T(8,128)(2,1)S(1)}, bf16[1,128,2048]{1,2,0:T(8,128)(2,1)}, u32[]{:S(2)}, u32[]{:S(2)}) collective-permute-start(bf16[1,128,2048]{1,2,0:T(8,128)(2,1)S(1)} %fusion.161), channel_id=1, source_target_pairs={{0,4},{4,8},{8,12},{12,16},{16,20},{20,24},{24,28},{28,32},{32,36}... | collective-permute-start | bytes 1572872 | tf_op jit(solution)/shard_map/ppermute | solution.py:14
  162.9 25.5 %collective-permute-start.5 = (bf16[1,128,2048]{1,2,0:T(8,128)(2,1)S(1)}, bf16[1,128,2048]{1,2,0:T(8,128)(2,1)}, u32[]{:S(2)}, u32[]{:S(2)}) collective-permute-start(bf16[1,128,2048]{1,2,0:T(8,128)(2,1)S(1)} %maximum_select_fusion), channel_id=1, source_target_pairs={{0,8},{4,12},{8,16},{12,20},{16,24},{20,28},{24,32},{28,36},{32,40... | collective-permute-start | bytes 1572872 | tf_op jit(solution)/shard_map/ppermute | solution.py:14
  233.6 27.5 %collective-permute-start.8 = (bf16[1,128,2048]{1,2,0:T(8,128)(2,1)S(1)}, bf16[1,128,2048]{1,2,0:T(8,128)(2,1)}, u32[]{:S(2)}, u32[]{:S(2)}) collective-permute-start(bf16[1,128,2048]{1,2,0:T(8,128)(2,1)S(1)} %maximum_select_fusion.1), channel_id=1, source_target_pairs={{0,16},{4,20},{8,24},{12,28},{16,32},{20,36},{24,40},{28,44},{32,4... | collective-permute-start | bytes 1572872 | tf_op jit(solution)/shard_map/ppermute | solution.py:14
  307.4 33.8 %collective-permute-start.11 = (bf16[1,128,2048]{1,2,0:T(8,128)(2,1)}, bf16[1,128,2048]{1,2,0:T(8,128)(2,1)}, u32[]{:S(2)}, u32[]{:S(2)}) collective-permute-start(bf16[1,128,2048]{1,2,0:T(8,128)(2,1)} %maximum_select_fusion.2), channel_id=1, source_target_pairs={{0,32},{4,36},{8,40},{12,44},{16,48},{20,52},{24,56},{28,60},{32,6... | collective-permute-start | bytes 1572872 | tf_op jit(solution)/shard_map/ppermute | solution.py:14
  310.9 78.1 %collective-permute-start.1 = (bf16[1,128,2048]{1,2,0:T(8,128)(2,1)}, bf16[1,128,2048]{1,2,0:T(8,128)(2,1)}, u32[]{:S(2)}, u32[]{:S(2)}) collective-permute-start(bf16[1,128,2048]{1,2,0:T(8,128)(2,1)} %get-tuple-element.1888), channel_id=1, source_target_pairs={{4,0},{8,4},{12,8},{16,12},{20,16},{24,20},{28,24},{32,28},{36,32}... | collective-permute-start | bytes 1572872 | tf_op jit(solution)/shard_map/ppermute | solution.py:14
  315.8 74.5 %collective-permute-start.3 = (bf16[1,128,2048]{1,2,0:T(8,128)(2,1)S(1)}, bf16[1,128,2048]{1,2,0:T(8,128)(2,1)}, u32[]{:S(2)}, u32[]{:S(2)}) collective-permute-start(bf16[1,128,2048]{1,2,0:T(8,128)(2,1)S(1)} %fusion.161), channel_id=1, source_target_pairs={{4,0},{8,4},{12,8},{16,12},{20,16},{24,20},{28,24},{32,28},{36,32}... | collective-permute-start | bytes 1572872 | tf_op jit(solution)/shard_map/ppermute | solution.py:14
  380.5 34.4 %collective-permute-start.6 = (bf16[1,128,2048]{1,2,0:T(8,128)(2,1)S(1)}, bf16[1,128,2048]{1,2,0:T(8,128)(2,1)}, u32[]{:S(2)}, u32[]{:S(2)}) collective-permute-start(bf16[1,128,2048]{1,2,0:T(8,128)(2,1)S(1)} %maximum_select_fusion), channel_id=1, source_target_pairs={{8,0},{12,4},{16,8},{20,12},{24,16},{28,20},{32,24},{36,28},{40,32... | collective-permute-start | bytes 1572872 | tf_op jit(solution)/shard_map/ppermute | solution.py:14
  381.8 33.1 %collective-permute-start.9 = (bf16[1,128,2048]{1,2,0:T(8,128)(2,1)S(1)}, bf16[1,128,2048]{1,2,0:T(8,128)(2,1)}, u32[]{:S(2)}, u32[]{:S(2)}) collective-permute-start(bf16[1,128,2048]{1,2,0:T(8,128)(2,1)S(1)} %maximum_select_fusion.1), channel_id=1, source_target_pairs={{16,0},{20,4},{24,8},{28,12},{32,16},{36,20},{40,24},{44,28},{48,3... | collective-permute-start | bytes 1572872 | tf_op jit(solution)/shard_map/ppermute | solution.py:14
  384.7 30.2 %collective-permute-start.12 = (bf16[1,128,2048]{1,2,0:T(8,128)(2,1)}, bf16[1,128,2048]{1,2,0:T(8,128)(2,1)}, u32[]{:S(2)}, u32[]{:S(2)}) collective-permute-start(bf16[1,128,2048]{1,2,0:T(8,128)(2,1)} %maximum_select_fusion.2), channel_id=1, source_target_pairs={{32,0},{36,4},{40,8},{44,12},{48,16},{52,20},{56,24},{60,28},{64,3... | collective-permute-start | bytes 1572872 | tf_op jit(solution)/shard_map/ppermute | solution.py:14
  389.0 25.9 %collective-permute-start.15 = (bf16[1,128,2048]{1,2,0:T(8,128)(2,1)}, bf16[1,128,2048]{1,2,0:T(8,128)(2,1)}, u32[]{:S(2)}, u32[]{:S(2)}) collective-permute-start(bf16[1,128,2048]{1,2,0:T(8,128)(2,1)} %maximum_select_fusion.3), channel_id=1, source_target_pairs={{64,0},{68,4},{72,8},{76,12},{80,16},{84,20},{88,24},{92,28},{96,3... | collective-permute-start | bytes 1572872 | tf_op jit(solution)/shard_map/ppermute | solution.py:14
  390.3 24.6 %collective-permute-start.14 = (bf16[1,128,2048]{1,2,0:T(8,128)(2,1)}, bf16[1,128,2048]{1,2,0:T(8,128)(2,1)}, u32[]{:S(2)}, u32[]{:S(2)}) collective-permute-start(bf16[1,128,2048]{1,2,0:T(8,128)(2,1)} %maximum_select_fusion.3), channel_id=1, source_target_pairs={{0,64},{4,68},{8,72},{12,76},{16,80},{20,84},{24,88},{28,92},{32,9... | collective-permute-start | bytes 1572872 | tf_op jit(solution)/shard_map/ppermute | solution.py:14
  857.6 14.6 %collective-permute-start.16 = (bf16[1,128,2048]{1,2,0:T(8,128)(2,1)}, bf16[1,128,2048]{1,2,0:T(8,128)(2,1)S(1)}, u32[]{:S(2)}, u32[]{:S(2)}) collective-permute-start(bf16[1,128,2048]{1,2,0:T(8,128)(2,1)} %scatter-add.44), channel_id=1, source_target_pairs={{64,0},{68,4},{72,8},{76,12},{80,16},{84,20},{88,24},{92,28},{96,3... | collective-permute-start | bytes 1572872 | tf_op jit(solution)/shard_map/ppermute | solution.py:14
  875.1 27.3 %collective-permute-start.20 = (bf16[1,128,2048]{1,2,0:T(8,128)(2,1)}, bf16[1,128,2048]{1,2,0:T(8,128)(2,1)}, u32[]{:S(2)}, u32[]{:S(2)}) collective-permute-start(bf16[1,128,2048]{1,2,0:T(8,128)(2,1)} %bitcast.41), channel_id=1, source_target_pairs={{0,32},{4,36},{8,40},{12,44},{16,48},{20,52},{24,56},{28,60},{32,6... | collective-permute-start | bytes 1572872 | tf_op jit(solution)/shard_map/ppermute | solution.py:14
  912.0 20.8 %collective-permute-start.21 = (bf16[1,64,2048]{1,2,0:T(8,128)(2,1)S(1)}, bf16[1,64,2048]{1,2,0:T(8,128)(2,1)S(1)}, u32[]{:S(2)}, u32[]{:S(2)}) collective-permute-start(bf16[1,64,2048]{1,2,0:T(8,128)(2,1)S(1)} %select_convert_fusion.2), channel_id=1, source_target_pairs={{0,16},{4,20},{8,24},{12,28},{16,0},{20,4},{24,8},{28,12},{32,48},... | collective-permute-start | bytes 786440 | tf_op jit(solution)/shard_map/ppermute | solution.py:18
  925.4 23.9 %collective-permute-start.23 = (bf16[1,128,2048]{1,2,0:T(8,128)(2,1)}, bf16[1,128,2048]{1,2,0:T(8,128)(2,1)}, u32[]{:S(2)}, u32[]{:S(2)}) collective-permute-start(bf16[1,128,2048]{1,2,0:T(8,128)(2,1)} %bitcast.46), channel_id=1, source_target_pairs={{0,16},{4,20},{8,24},{12,28},{16,32},{20,36},{24,40},{28,44},{32,4... | collective-permute-start | bytes 1572872 | tf_op jit(solution)/shard_map/ppermute | solution.py:14
  960.3 15.9 %collective-permute-start.24 = (bf16[1,64,2048]{1,2,0:T(8,128)(2,1)S(1)}, bf16[1,64,2048]{1,2,0:T(8,128)(2,1)S(1)}, u32[]{:S(2)}, u32[]{:S(2)}) collective-permute-start(bf16[1,64,2048]{1,2,0:T(8,128)(2,1)S(1)} %select_convert_fusion.1), channel_id=1, source_target_pairs={{0,8},{4,12},{8,0},{12,4},{16,24},{20,28},{24,16},{28,20},{32,40},... | collective-permute-start | bytes 786440 | tf_op jit(solution)/shard_map/ppermute | solution.py:18
  969.7 31.8 %collective-permute-start.26 = (bf16[1,128,2048]{1,2,0:T(8,128)(2,1)S(1)}, bf16[1,128,2048]{1,2,0:T(8,128)(2,1)}, u32[]{:S(2)}, u32[]{:S(2)}) collective-permute-start(bf16[1,128,2048]{1,2,0:T(8,128)(2,1)S(1)} %bitcast.1723), channel_id=1, source_target_pairs={{0,8},{4,12},{8,16},{12,20},{16,24},{20,28},{24,32},{28,36},{32,40... | collective-permute-start | bytes 1572872 | tf_op jit(solution)/shard_map/ppermute | solution.py:14
  1009.6 41.9 %collective-permute-start.27 = (bf16[1,64,2048]{1,2,0:T(8,128)(2,1)}, bf16[1,64,2048]{1,2,0:T(8,128)(2,1)}, u32[]{:S(2)}, u32[]{:S(2)}) collective-permute-start(bf16[1,64,2048]{1,2,0:T(8,128)(2,1)} %select_convert_fusion), channel_id=1, source_target_pairs={{0,4},{4,0},{8,12},{12,8},{16,20},{20,16},{24,28},{28,24},{32,36},... | collective-permute-start | bytes 786440 | tf_op jit(solution)/shard_map/ppermute | solution.py:18
  1042.5 37.8 %collective-permute-start.28 = (bf16[1,128,2048]{1,2,0:T(8,128)(2,1)}, bf16[1,128,2048]{1,2,0:T(8,128)(2,1)}, u32[]{:S(2)}, u32[]{:S(2)}) collective-permute-start(bf16[1,128,2048]{1,2,0:T(8,128)(2,1)} %copy.1124), channel_id=1, source_target_pairs={{0,4},{4,8},{8,12},{12,16},{16,20},{20,24},{24,28},{28,32},{32,36}... | collective-permute-start | bytes 1572872 | tf_op jit(solution)/shard_map/ppermute | solution.py:14
  1064.9 15.4 %collective-permute-start.29 = (bf16[1,128,2048]{1,2,0:T(8,128)(2,1)}, bf16[1,128,2048]{1,2,0:T(8,128)(2,1)}, u32[]{:S(2)}, u32[]{:S(2)}) collective-permute-start(bf16[1,128,2048]{1,2,0:T(8,128)(2,1)} %scatter-add.50), channel_id=1, source_target_pairs={{4,0},{8,4},{12,8},{16,12},{20,16},{24,20},{28,24},{32,28},{36,32}... | collective-permute-start | bytes 1572872 | tf_op jit(solution)/shard_map/ppermute | solution.py:14
  1071.4 29.8 %collective-permute-start.30 = (bf16[1,128,2048]{2,1,0:T(8,128)(2,1)}, bf16[1,128,2048]{2,1,0:T(8,128)(2,1)}, u32[]{:S(2)}, u32[]{:S(2)}) collective-permute-start(bf16[1,128,2048]{2,1,0:T(8,128)(2,1)} %copy.823), channel_id=1, source_target_pairs={{0,4},{4,8},{8,12},{12,16},{16,20},{20,24},{24,28},{28,32},{32,36}... | collective-permute-start | bytes 1572872 | tf_op jit(solution)/shard_map/ppermute | solution.py:14
  1097.3 137.7 %collective-permute-start.31 = (bf16[1,128,2048]{2,1,0:T(8,128)(2,1)S(1)}, bf16[1,128,2048]{2,1,0:T(8,128)(2,1)S(1)}, u32[]{:S(2)}, u32[]{:S(2)}) collective-permute-start(bf16[1,128,2048]{2,1,0:T(8,128)(2,1)S(1)} %copy.824), channel_id=1, source_target_pairs={{4,0},{8,4},{12,8},{16,12},{20,16},{24,20},{28,24},{32,28},{36,32}... | collective-permute-start | bytes 1572872 | tf_op jit(solution)/shard_map/ppermute | solution.py:14
  (260 other events, 4159.7 us)
Sparse Core Ops, SparseCore 0:
  1084.6 147.5 all-reduce.23
where the time goes:
time: 1260 us; the launch traced here: 1240 us
  local copies, waits for them, and re-layouts  460 us (37%)
  matrix products  290 us (23%)
  waiting for transfers between devices  207 us (16%)
  other arithmetic  151 us (12%)
  starting transfers between devices  117 us (9%)
  between operations  16 us (1%)
    slice x15, local copies, waits for them, and re-layouts, coarsen(): extended[:, offset:offset + 2 * out_rows:2].astype(jnp.float32)  198 us
    psum x1, waiting for transfers between devices, per_device(): lax.psum(jnp.stack(weight_grads), ('seq', 'dp'))  130 us
    dot_general x52, matrix products, head_group(): jnp.einsum('bnrqhe,bnkhe->bnrhqk', q_view, key_blocks[..., 0, :], preferr...  75.9 us
    ppermute x24, starting transfers between devices, passed_along(): lax.ppermute(value, axis, [(source, source + steps) for source in range(i...  72 us
    slice x5, local copies, waits for them, and re-layouts, coarsen(): summed = weight[0] * extended[:, 0:2 * out_rows:2].astype(jnp.float32)  68.5 us
    dot_general x52, matrix products, head_group(): jnp.einsum('bnrhqk,bnkhe->bnrqhe', p_slice, key_blocks[..., 1, :], prefer...  50.2 us
    dot_general x52, matrix products, head_group(): jnp.einsum('bnrqhe,bnkhe->bnrhqk', do_view, key_blocks[..., 1, :], prefer...  45.6 us
    ppermute x8, waiting for transfers between devices, partner_2(): lax.ppermute(array, axis, [(i, i ^ 1 << distance) for i in range(lax.axis...  45.3 us
  transfers between devices with their start and end apart: 33, of which 13 were waited for; matrix products, arithmetic and copies ran while one was open for 25% of the time, Pallas kernels for 0%

commit v1 on v0

--- a/solution.py
+++ b/solution.py
@@ -333,7 +333,7 @@
     grad_value = (
         grad_pairs[:, :, :, 1, :].reshape(seqs_dev, tok_rows, feat_width).astype(jnp.bfloat16)
     )
-    weight_sum = lax.psum(jnp.stack(weight_grads), ("seq", "dp")).reshape(
+    weight_sum = jnp.sum(lax.all_gather(jnp.stack(weight_grads), ("seq", "dp")), axis=0).reshape(
         levels, 4, head_count, 2, head_size
     )
     grad_conv_key = weight_sum[:, :, :, 0, :].reshape(levels, 4, feat_width)

time: 1260 us -> 1220 us (0.968)
  waiting for transfers between devices: 207 us -> 136 us
  matrix products: 290 us -> 314 us
  local copies, waits for them, and re-layouts: 460 us -> 482 us
  other arithmetic: 151 us -> 134 us
    psum x1 -> x0, waiting for transfers between devices: 130 us -> none  [per_device(): lax.psum(jnp.stack(weight_grads), ('seq', 'dp'))]
    all_gather x0 -> x1, waiting for transfers between devices: none -> 52.9 us  [per_device(): lax.all_gather(jnp.stack(weight_grads), ('seq', 'dp'))]
    dot_general x52, matrix products: 45.6 us -> 92.5 us  [head_group(): jnp.einsum('bnrqhe,bnkhe->bnrhqk', do_view, key_blocks[..., 1, :], prefer...]
    dot_general x52, matrix products: 37.6 us -> 11.9 us  [head_group(): jnp.einsum('bnrhqk,bnrqhe->bnkhe', p_slice, do_view, preferred_element_ty...]
    while x360 -> x128, local copies, waits for them, and re-layouts: 14.6 us -> 33.8 us
    dot_general x52, matrix products: 35.7 us -> 22.6 us  [head_group(): jnp.einsum('bnrhqk,bnrqhe->bnkhe', ds_slice, q_view, preferred_element_ty...]
    unnamed x189 -> x195, local copies, waits for them, and re-layouts: 33.6 us -> 37.7 us
  transfers between devices with their start and end apart: 33 -> 33, of which waited for: 13 -> 14; matrix products, arithmetic and copies ran while one was open for 25% -> 25% of each run, Pallas kernels for 0% -> 0%
where the time goes in v1:
time: 1220 us; the launch traced here: 1200 us
  local copies, waits for them, and re-layouts  482 us (40%)
  matrix products  314 us (26%)
  waiting for transfers between devices  136 us (11%)
  other arithmetic  134 us (11%)
  starting transfers between devices  118 us (10%)
  between operations  16 us (1%)
    slice x15, local copies, waits for them, and re-layouts, coarsen(): extended[:, offset:offset + 2 * out_rows:2].astype(jnp.float32)  199 us
    dot_general x52, matrix products, head_group(): jnp.einsum('bnrqhe,bnkhe->bnrhqk', do_view, key_blocks[..., 1, :], prefer...  92.5 us
    dot_general x52, matrix products, head_group(): jnp.einsum('bnrqhe,bnkhe->bnrhqk', q_view, key_blocks[..., 0, :], preferr...  88 us
    ppermute x24, starting transfers between devices, passed_along(): lax.ppermute(value, axis, [(source, source + steps) for source in range(i...  73.4 us
    slice x5, local copies, waits for them, and re-layouts, coarsen(): summed = weight[0] * extended[:, 0:2 * out_rows:2].astype(jnp.float32)  67.6 us
    all_gather x1, waiting for transfers between devices, per_device(): lax.all_gather(jnp.stack(weight_grads), ('seq', 'dp'))  52.9 us
    dot_general x52, matrix products, head_group(): jnp.einsum('bnrhqk,bnkhe->bnrqhe', ds_slice, key_blocks[..., 0, :], prefe...  51.6 us
    dot_general x52, matrix products, head_group(): jnp.einsum('bnrhqk,bnkhe->bnrqhe', p_slice, key_blocks[..., 1, :], prefer...  47.7 us
  transfers between devices with their start and end apart: 33, of which 14 were waited for; matrix products, arithmetic and copies ran while one was open for 25% of the time, Pallas kernels for 0%

profile of v1, /device:TPU:1, one launch (start us, length us, event | category | flops | bytes accessed | tf_op | source)
XLA Modules:
  0.0 1203.0 jit_solution(667915682794034222)
XLA Ops:
  15.2 20.2 %slice.1813 = bf16[1,128,2048]{1,2,0:T(8,128)(2,1)S(1)} slice(bf16[1,256,2048]{1,2,0:T(8,128)(2,1)S(1)} %bitcast.1717), slice={[0:1:1], [0:256:2], [0:2048:1]} | slice | bytes 1048576 | tf_op jit(solution)/shard_map/slice | solution.py:25
  35.5 20.2 %slice.1815 = bf16[1,128,2048]{1,2,0:T(8,128)(2,1)S(1)} slice(bf16[1,256,2048]{1,2,0:T(8,128)(2,1)S(1)} %bitcast.1718), slice={[0:1:1], [1:256:2], [0:2048:1]} | slice | bytes 1048576 | tf_op jit(solution)/shard_map/slice | solution.py:25
  58.7 20.9 %slice.1809 = bf16[1,128,2048]{1,2,0:T(8,128)(2,1)S(1)} slice(bf16[1,258,2048]{1,2,0:T(8,128)(2,1)} %pad_maximum_fusion.14), slice={[0:1:1], [0:256:2], [0:2048:1]} | slice | bytes 1048576 | tf_op jit(solution)/shard_map/slice | solution.py:23
  79.6 21.4 %slice.1811 = bf16[1,128,2048]{1,2,0:T(8,128)(2,1)} slice(bf16[1,258,2048]{1,2,0:T(8,128)(2,1)} %pad_maximum_fusion.14), slice={[0:1:1], [1:257:2], [0:2048:1]} | slice | bytes 1048576 | tf_op jit(solution)/shard_map/slice | solution.py:25
  117.0 11.0 slice.1824
  130.9 11.4 slice.1818
  142.4 12.1 %slice.1820 = bf16[1,64,2048]{1,2,0:T(8,128)(2,1)} slice(bf16[1,130,2048]{1,2,0:T(8,128)(2,1)} %pad_maximum_fusion.17), slice={[0:1:1], [1:129:2], [0:2048:1]} | slice | bytes 524288 | tf_op jit(solution)/shard_map/slice | solution.py:25
  177.7 11.0 slice.1833
  191.6 11.8 slice.1827
  203.4 11.9 slice.1829
  219.3 12.9 %collective-permute-done.7 = bf16[1,64,2048]{1,2,0:T(8,128)(2,1)S(1)} collective-permute-done((bf16[1,64,2048]{1,2,0:T(8,128)(2,1)}, bf16[1,64,2048]{1,2,0:T(8,128)(2,1)S(1)}, u32[]{:S(2)}, u32[]{:S(2)}) %collective-permute-start.7) | collective-permute-done | bytes 262176 | tf_op jit(solution)/shard_map/ppermute | solution.py:18
  249.8 11.3 slice.1842
  263.9 11.8 slice.1836
  275.6 11.9 slice.1838
  292.3 12.7 %collective-permute-done.10 = bf16[1,64,2048]{1,2,0:T(8,128)(2,1)S(1)} collective-permute-done((bf16[1,64,2048]{1,2,0:T(8,128)(2,1)}, bf16[1,64,2048]{1,2,0:T(8,128)(2,1)S(1)}, u32[]{:S(2)}, u32[]{:S(2)}) %collective-permute-start.10) | collective-permute-done | bytes 262176 | tf_op jit(solution)/shard_map/ppermute | solution.py:18
  318.1 11.4 slice.1849
  329.5 11.9 slice.1851
  345.1 11.8 slice.1845
  356.9 11.9 slice.1847
  430.6 446.4 %while.137 = (s32[]{:T(128)}, bf16[1,2,128,8,128]{4,3,2,1,0:T(8,128)(2,1)}, bf16[1,2,128,8,128]{4,3,2,1,0:T(8,128)(2,1)}, f32[1,4,128,8,2,128]{5,4,3,0,2,1:T(2,1...) while((s32[]{:T(128)}, ...), condition=%wide.region_16.17_spmd.clone.clone, body=%wide.region_0.16_spmd.clone.clone.sunk | while | flops 1327627008 | bytes 128404528 | solution.py:269
  939.0 13.6 %collective-permute-start.21 = (bf16[1,64,2048]{1,2,0:T(8,128)(2,1)S(1)}, bf16[1,64,2048]{1,2,0:T(8,128)(2,1)S(1)}, u32[]{:S(2)}, u32[]{:S(2)}) collective-permute-start(bf16[1,64,2048]{1,2,0:T(8,128)(2,1)S(1)} %select_convert_fusion.2), channel_id=1, source_target_pairs={{0,16},{4,20},{8,24},{12,28},{16,0},{20,4},{24,8},{28,12},{32,48},... | collective-permute-start | bytes 786440 | tf_op jit(solution)/shard_map/ppermute | solution.py:18
  1029.6 17.7 %collective-permute-start.27 = (bf16[1,64,2048]{1,2,0:T(8,128)(2,1)}, bf16[1,64,2048]{1,2,0:T(8,128)(2,1)}, u32[]{:S(2)}, u32[]{:S(2)}) collective-permute-start(bf16[1,64,2048]{1,2,0:T(8,128)(2,1)} %select_convert_fusion), channel_id=1, source_target_pairs={{0,4},{4,0},{8,12},{12,8},{16,20},{20,16},{24,28},{28,24},{32,36},... | collective-permute-start | bytes 786440 | tf_op jit(solution)/shard_map/ppermute | solution.py:18
  1130.2 52.9 %all-gather.3.cloned.1.call-done = f32[640,4,2048]{2,1,0:T(4,128)} async-done(((f32[5,4,2048]{2,1,0:T(4,128)}), f32[640,4,2048]{2,1,0:T(4,128)}) %all-gather.3.cloned.1.call-update) | async-done | bytes 20971536 | tf_op jit(solution)/shard_map/all_gather | solution.py:336
  1183.0 10.9 reduce_sum.231
  (970 shorter events, 829.5 us)
Async XLA Ops:
  7.2 1175.9 %all-gather.3.cloned.1.call-start = ((), (), s32[]{:S(2)}) async-start(), calls=%async_computation | async-start | bytes 21135360 | tf_op jit(solution)/shard_map/all_gather | solution.py:336
  10.7 45.3 %collective-permute-start = (bf16[1,128,2048]{1,2,0:T(8,128)(2,1)S(1)}, bf16[1,128,2048]{1,2,0:T(8,128)(2,1)S(1)}, u32[]{:S(2)}, u32[]{:S(2)}) collective-permute-start(bf16[1,128,2048]{1,2,0:T(8,128)(2,1)S(1)} %get-tuple-element.1887), channel_id=1, source_target_pairs={{0,4},{4,8},{8,12},{12,16},{16,20},{20,24},{24,28},{28,32},{32,36}... | collective-permute-start | bytes 1572872 | tf_op jit(solution)/shard_map/ppermute | solution.py:14
  103.9 24.1 %collective-permute-start.2 = (bf16[1,128,2048]{1,2,0:T(8,128)(2,1)S(1)}, bf16[1,128,2048]{1,2,0:T(8,128)(2,1)}, u32[]{:S(2)}, u32[]{:S(2)}) collective-permute-start(bf16[1,128,2048]{1,2,0:T(8,128)(2,1)S(1)} %fusion.161), channel_id=1, source_target_pairs={{0,4},{4,8},{8,12},{12,16},{16,20},{20,24},{24,28},{28,32},{32,36}... | collective-permute-start | bytes 1572872 | tf_op jit(solution)/shard_map/ppermute | solution.py:14
  163.0 25.7 %collective-permute-start.5 = (bf16[1,128,2048]{1,2,0:T(8,128)(2,1)S(1)}, bf16[1,128,2048]{1,2,0:T(8,128)(2,1)}, u32[]{:S(2)}, u32[]{:S(2)}) collective-permute-start(bf16[1,128,2048]{1,2,0:T(8,128)(2,1)S(1)} %maximum_select_fusion), channel_id=1, source_target_pairs={{0,8},{4,12},{8,16},{12,20},{16,24},{20,28},{24,32},{28,36},{32,40... | collective-permute-start | bytes 1572872 | tf_op jit(solution)/shard_map/ppermute | solution.py:14
  234.0 27.2 %collective-permute-start.8 = (bf16[1,128,2048]{1,2,0:T(8,128)(2,1)S(1)}, bf16[1,128,2048]{1,2,0:T(8,128)(2,1)}, u32[]{:S(2)}, u32[]{:S(2)}) collective-permute-start(bf16[1,128,2048]{1,2,0:T(8,128)(2,1)S(1)} %maximum_select_fusion.1), channel_id=1, source_target_pairs={{0,16},{4,20},{8,24},{12,28},{16,32},{20,36},{24,40},{28,44},{32,4... | collective-permute-start | bytes 1572872 | tf_op jit(solution)/shard_map/ppermute | solution.py:14
  307.6 33.8 %collective-permute-start.11 = (bf16[1,128,2048]{1,2,0:T(8,128)(2,1)}, bf16[1,128,2048]{1,2,0:T(8,128)(2,1)}, u32[]{:S(2)}, u32[]{:S(2)}) collective-permute-start(bf16[1,128,2048]{1,2,0:T(8,128)(2,1)} %maximum_select_fusion.2), channel_id=1, source_target_pairs={{0,32},{4,36},{8,40},{12,44},{16,48},{20,52},{24,56},{28,60},{32,6... | collective-permute-start | bytes 1572872 | tf_op jit(solution)/shard_map/ppermute | solution.py:14
  311.1 81.6 %collective-permute-start.1 = (bf16[1,128,2048]{1,2,0:T(8,128)(2,1)}, bf16[1,128,2048]{1,2,0:T(8,128)(2,1)}, u32[]{:S(2)}, u32[]{:S(2)}) collective-permute-start(bf16[1,128,2048]{1,2,0:T(8,128)(2,1)} %get-tuple-element.1888), channel_id=1, source_target_pairs={{4,0},{8,4},{12,8},{16,12},{20,16},{24,20},{28,24},{32,28},{36,32}... | collective-permute-start | bytes 1572872 | tf_op jit(solution)/shard_map/ppermute | solution.py:14
  316.0 86.7 %collective-permute-start.3 = (bf16[1,128,2048]{1,2,0:T(8,128)(2,1)S(1)}, bf16[1,128,2048]{1,2,0:T(8,128)(2,1)}, u32[]{:S(2)}, u32[]{:S(2)}) collective-permute-start(bf16[1,128,2048]{1,2,0:T(8,128)(2,1)S(1)} %fusion.161), channel_id=1, source_target_pairs={{4,0},{8,4},{12,8},{16,12},{20,16},{24,20},{28,24},{32,28},{36,32}... | collective-permute-start | bytes 1572872 | tf_op jit(solution)/shard_map/ppermute | solution.py:14
  372.8 15.6 %collective-permute-start.13 = (bf16[1,64,2048]{1,2,0:T(8,128)(2,1)}, bf16[1,64,2048]{1,2,0:T(8,128)(2,1)}, u32[]{:S(2)}, u32[]{:S(2)}) collective-permute-start(bf16[1,64,2048]{1,2,0:T(8,128)(2,1)} %fusion.193), channel_id=1, source_target_pairs={{0,32},{4,36},{8,40},{12,44},{16,48},{20,52},{24,56},{28,60},{32,0... | collective-permute-start | bytes 786440 | tf_op jit(solution)/shard_map/ppermute | solution.py:18
  385.8 33.6 %collective-permute-start.6 = (bf16[1,128,2048]{1,2,0:T(8,128)(2,1)S(1)}, bf16[1,128,2048]{1,2,0:T(8,128)(2,1)}, u32[]{:S(2)}, u32[]{:S(2)}) collective-permute-start(bf16[1,128,2048]{1,2,0:T(8,128)(2,1)S(1)} %maximum_select_fusion), channel_id=1, source_target_pairs={{8,0},{12,4},{16,8},{20,12},{24,16},{28,20},{32,24},{36,28},{40,32... | collective-permute-start | bytes 1572872 | tf_op jit(solution)/shard_map/ppermute | solution.py:14
  387.1 32.4 %collective-permute-start.9 = (bf16[1,128,2048]{1,2,0:T(8,128)(2,1)S(1)}, bf16[1,128,2048]{1,2,0:T(8,128)(2,1)}, u32[]{:S(2)}, u32[]{:S(2)}) collective-permute-start(bf16[1,128,2048]{1,2,0:T(8,128)(2,1)S(1)} %maximum_select_fusion.1), channel_id=1, source_target_pairs={{16,0},{20,4},{24,8},{28,12},{32,16},{36,20},{40,24},{44,28},{48,3... | collective-permute-start | bytes 1572872 | tf_op jit(solution)/shard_map/ppermute | solution.py:14
  388.4 31.1 %collective-permute-start.12 = (bf16[1,128,2048]{1,2,0:T(8,128)(2,1)}, bf16[1,128,2048]{1,2,0:T(8,128)(2,1)}, u32[]{:S(2)}, u32[]{:S(2)}) collective-permute-start(bf16[1,128,2048]{1,2,0:T(8,128)(2,1)} %maximum_select_fusion.2), channel_id=1, source_target_pairs={{32,0},{36,4},{40,8},{44,12},{48,16},{52,20},{56,24},{60,28},{64,3... | collective-permute-start | bytes 1572872 | tf_op jit(solution)/shard_map/ppermute | solution.py:14
  392.7 26.8 %collective-permute-start.14 = (bf16[1,128,2048]{1,2,0:T(8,128)(2,1)}, bf16[1,128,2048]{1,2,0:T(8,128)(2,1)}, u32[]{:S(2)}, u32[]{:S(2)}) collective-permute-start(bf16[1,128,2048]{1,2,0:T(8,128)(2,1)} %maximum_select_fusion.3), channel_id=1, source_target_pairs={{0,64},{4,68},{8,72},{12,76},{16,80},{20,84},{24,88},{28,92},{32,9... | collective-permute-start | bytes 1572872 | tf_op jit(solution)/shard_map/ppermute | solution.py:14
  402.6 16.9 %collective-permute-start.15 = (bf16[1,128,2048]{1,2,0:T(8,128)(2,1)}, bf16[1,128,2048]{1,2,0:T(8,128)(2,1)}, u32[]{:S(2)}, u32[]{:S(2)}) collective-permute-start(bf16[1,128,2048]{1,2,0:T(8,128)(2,1)} %maximum_select_fusion.3), channel_id=1, source_target_pairs={{64,0},{68,4},{72,8},{76,12},{80,16},{84,20},{88,24},{92,28},{96,3... | collective-permute-start | bytes 1572872 | tf_op jit(solution)/shard_map/ppermute | solution.py:14
  884.2 15.4 %collective-permute-start.16 = (bf16[1,128,2048]{1,2,0:T(8,128)(2,1)}, bf16[1,128,2048]{1,2,0:T(8,128)(2,1)S(1)}, u32[]{:S(2)}, u32[]{:S(2)}) collective-permute-start(bf16[1,128,2048]{1,2,0:T(8,128)(2,1)} %scatter-add.44), channel_id=1, source_target_pairs={{64,0},{68,4},{72,8},{76,12},{80,16},{84,20},{88,24},{92,28},{96,3... | collective-permute-start | bytes 1572872 | tf_op jit(solution)/shard_map/ppermute | solution.py:14
  885.6 14.6 %collective-permute-start.17 = (bf16[1,128,2048]{1,2,0:T(8,128)(2,1)S(1)}, bf16[1,128,2048]{1,2,0:T(8,128)(2,1)S(1)}, u32[]{:S(2)}, u32[]{:S(2)}) collective-permute-start(bf16[1,128,2048]{1,2,0:T(8,128)(2,1)S(1)} %bitcast.1760), channel_id=1, source_target_pairs={{0,64},{4,68},{8,72},{12,76},{16,80},{20,84},{24,88},{28,92},{32,9... | collective-permute-start | bytes 1572872 | tf_op jit(solution)/shard_map/ppermute | solution.py:14
  901.7 27.7 %collective-permute-start.20 = (bf16[1,128,2048]{1,2,0:T(8,128)(2,1)}, bf16[1,128,2048]{1,2,0:T(8,128)(2,1)}, u32[]{:S(2)}, u32[]{:S(2)}) collective-permute-start(bf16[1,128,2048]{1,2,0:T(8,128)(2,1)} %bitcast.41), channel_id=1, source_target_pairs={{0,32},{4,36},{8,40},{12,44},{16,48},{20,52},{24,56},{28,60},{32,6... | collective-permute-start | bytes 1572872 | tf_op jit(solution)/shard_map/ppermute | solution.py:14
  939.0 21.0 %collective-permute-start.21 = (bf16[1,64,2048]{1,2,0:T(8,128)(2,1)S(1)}, bf16[1,64,2048]{1,2,0:T(8,128)(2,1)S(1)}, u32[]{:S(2)}, u32[]{:S(2)}) collective-permute-start(bf16[1,64,2048]{1,2,0:T(8,128)(2,1)S(1)} %select_convert_fusion.2), channel_id=1, source_target_pairs={{0,16},{4,20},{8,24},{12,28},{16,0},{20,4},{24,8},{28,12},{32,48},... | collective-permute-start | bytes 786440 | tf_op jit(solution)/shard_map/ppermute | solution.py:18
  952.7 23.8 %collective-permute-start.23 = (bf16[1,128,2048]{1,2,0:T(8,128)(2,1)}, bf16[1,128,2048]{1,2,0:T(8,128)(2,1)}, u32[]{:S(2)}, u32[]{:S(2)}) collective-permute-start(bf16[1,128,2048]{1,2,0:T(8,128)(2,1)} %bitcast.46), channel_id=1, source_target_pairs={{0,16},{4,20},{8,24},{12,28},{16,32},{20,36},{24,40},{28,44},{32,4... | collective-permute-start | bytes 1572872 | tf_op jit(solution)/shard_map/ppermute | solution.py:14
  987.6 16.0 %collective-permute-start.24 = (bf16[1,64,2048]{1,2,0:T(8,128)(2,1)S(1)}, bf16[1,64,2048]{1,2,0:T(8,128)(2,1)S(1)}, u32[]{:S(2)}, u32[]{:S(2)}) collective-permute-start(bf16[1,64,2048]{1,2,0:T(8,128)(2,1)S(1)} %select_convert_fusion.1), channel_id=1, source_target_pairs={{0,8},{4,12},{8,0},{12,4},{16,24},{20,28},{24,16},{28,20},{32,40},... | collective-permute-start | bytes 786440 | tf_op jit(solution)/shard_map/ppermute | solution.py:18
  997.1 22.2 %collective-permute-start.26 = (bf16[1,128,2048]{1,2,0:T(8,128)(2,1)}, bf16[1,128,2048]{1,2,0:T(8,128)(2,1)}, u32[]{:S(2)}, u32[]{:S(2)}) collective-permute-start(bf16[1,128,2048]{1,2,0:T(8,128)(2,1)} %bitcast.51), channel_id=1, source_target_pairs={{0,8},{4,12},{8,16},{12,20},{16,24},{20,28},{24,32},{28,36},{32,40... | collective-permute-start | bytes 1572872 | tf_op jit(solution)/shard_map/ppermute | solution.py:14
  1029.6 33.0 %collective-permute-start.27 = (bf16[1,64,2048]{1,2,0:T(8,128)(2,1)}, bf16[1,64,2048]{1,2,0:T(8,128)(2,1)}, u32[]{:S(2)}, u32[]{:S(2)}) collective-permute-start(bf16[1,64,2048]{1,2,0:T(8,128)(2,1)} %select_convert_fusion), channel_id=1, source_target_pairs={{0,4},{4,0},{8,12},{12,8},{16,20},{20,16},{24,28},{28,24},{32,36},... | collective-permute-start | bytes 786440 | tf_op jit(solution)/shard_map/ppermute | solution.py:18
  1058.2 28.0 %collective-permute-start.28 = (bf16[1,128,2048]{1,2,0:T(8,128)(2,1)}, bf16[1,128,2048]{1,2,0:T(8,128)(2,1)}, u32[]{:S(2)}, u32[]{:S(2)}) collective-permute-start(bf16[1,128,2048]{1,2,0:T(8,128)(2,1)} %copy.1125), channel_id=1, source_target_pairs={{0,4},{4,8},{8,12},{12,16},{16,20},{20,24},{24,28},{28,32},{32,36}... | collective-permute-start | bytes 1572872 | tf_op jit(solution)/shard_map/ppermute | solution.py:14
  1098.6 22.2 %collective-permute-start.30 = (bf16[1,128,2048]{2,1,0:T(8,128)(2,1)}, bf16[1,128,2048]{2,1,0:T(8,128)(2,1)}, u32[]{:S(2)}, u32[]{:S(2)}) collective-permute-start(bf16[1,128,2048]{2,1,0:T(8,128)(2,1)} %copy.823), channel_id=1, source_target_pairs={{0,4},{4,8},{8,12},{12,16},{16,20},{20,24},{24,28},{28,32},{32,36}... | collective-permute-start | bytes 1572872 | tf_op jit(solution)/shard_map/ppermute | solution.py:14
  (147 other events, 3368.9 us)
Sparse Core Ops, SparseCore 0:
  1090.8 92.1 all-gather.2
